TPU v7x, 32 devices: a whole 2x2x4 slice. The times are simulated.
32 devices in a mesh: seq: 8 (over z, y), kvh: 4 (over x, core).
Axes of the slice: x: 2, y: 2, z: 4, core: 2. Of those that a mesh axis runs over, the one named last changes fastest.
Arguments:
- queries: bfloat16 [2048, 4096], P(('seq', 'kvh')), may hold values from -8 to 8
- keys: bfloat16 [2048, 2048], P(('seq', 'kvh')), may hold values from -8 to 8
- values: bfloat16 [2048, 2048], P(('seq', 'kvh')), may hold values from -6 to 6
- out_grad: bfloat16 [2048, 4096], P(('seq', 'kvh')), may hold values from -6 to 6
- file_start: int32 [2048], P('seq'), may hold values from 0 to 2047, as said below
Outputs:
- attn_out: bfloat16 [2048, 4096], P(('seq', 'kvh'))
- query_grad: bfloat16 [2048, 4096], P(('seq', 'kvh'))
- key_gradient: bfloat16 [2048, 2048], P(('seq', 'kvh'))
- value_gradient: bfloat16 [2048, 2048], P(('seq', 'kvh'))
Inputs may be any that keep to these rules, and one draw needn't show every extreme that they name: `file_start`: entries never fall along the slab; each entry is at most its own token's position, and equals it at the first token of a file; the first file starts at 0 and the slab's last token begins a file of its own.
All inputs are finite; a program needn't handle non-finite values.
Results may differ from a plain program's by a relative error of at most 0.024.
Values may be sent and summed in bfloat16 or wider, within the bound.
A program may use at most 128 MiB of HBM per device.

v0:
```python
import jax
import jax.numpy as jnp
from jax import lax
from jax.sharding import PartitionSpec as P

HEAD_SIZE = 128
WINDOW_TOKENS = 1024


score_scale = 168.0 ** (-0.5)


def shifted(value, axis, steps):
    count = lax.axis_size(axis)
    leading, last = (max(0, -steps), min(count, count - steps))
    return lax.ppermute(value, axis, [(source, source + steps) for source in range(leading, last)])


def product(einsum_form, left_side, right_side, factor):
    return (
        jnp.einsum(einsum_form, left_side, right_side, preferred_element_type=jnp.float32) * factor
    )


def masked_scores(query_head, key_block, query_pos, lower_key, key_spots):
    raw_scores = (
        jnp.einsum("qrd,kd->rqk", query_head, key_block, preferred_element_type=jnp.float32)
        * score_scale
    )
    allowed = (key_spots[None, :] >= lower_key[:, None]) & (
        key_spots[None, :] <= query_pos[:, None]
    )
    return jnp.where(allowed[None], raw_scores, -jnp.inf)


def head_pass(query_head, grad_head, key_blocks, value_blocks, key_positions, query_pos, lower_key):
    row_count, group_width, head_dim = query_head.shape
    block_width = key_blocks[0].shape[0]
    last_block = len(key_blocks) - 1
    row_fill = jnp.zeros((row_count, group_width, head_dim), jnp.float32)
    score_parts = []
    for block_index in range(last_block + 1):
        score_parts.append(
            masked_scores(
                query_head,
                key_blocks[block_index],
                query_pos,
                lower_key,
                key_positions[block_index],
            )
        )
    scores = jnp.concatenate(score_parts, axis=2)
    row_peak = jnp.max(scores, axis=2, keepdims=True)
    log_total = row_peak + jnp.log(jnp.sum(jnp.exp(scores - row_peak), axis=2, keepdims=True))
    prob_full = jnp.exp(scores - log_total)
    prob_low = prob_full.astype(jnp.bfloat16)
    attention = row_fill
    for block_index in range(last_block + 1):
        low_block = prob_low[:, :, block_index * block_width : (block_index + 1) * block_width]
        attention = attention + product("rqk,kd->qrd", low_block, value_blocks[block_index], 1.0)
    attn_low = attention.astype(jnp.bfloat16)
    row_delta = jnp.transpose(
        jnp.sum(grad_head.astype(jnp.float32) * attn_low.astype(jnp.float32), axis=2)
    )
    query_grad = row_fill
    key_grads = []
    value_grads = []
    for block_index in range(last_block + 1):
        full_block = prob_full[:, :, block_index * block_width : (block_index + 1) * block_width]
        low_block = prob_low[:, :, block_index * block_width : (block_index + 1) * block_width]
        prob_grad = product("qrd,kd->rqk", grad_head, value_blocks[block_index], 1.0)
        score_grad = (full_block * (prob_grad - row_delta[:, :, None])).astype(jnp.bfloat16)
        query_grad = query_grad + product(
            "rqk,kd->qrd", score_grad, key_blocks[block_index], score_scale
        )
        key_grads.append(product("rqk,qrd->kd", score_grad, query_head, score_scale))
        value_grads.append(product("rqk,qrd->kd", low_block, grad_head, 1.0))
    return (
        attn_low,
        query_grad.astype(jnp.bfloat16),
        log_total[:, :, 0],
        row_delta,
        key_grads,
        value_grads,
    )


def body(queries, keys, values, out_grad, file_start):
    query_row_slice, key_row_slice, value_rows, grad_rows = (
        lax.all_to_all(queries, "kvh", split_axis=1, concat_axis=0, tiled=True),
        lax.all_to_all(keys, "kvh", split_axis=1, concat_axis=0, tiled=True),
        lax.all_to_all(values, "kvh", split_axis=1, concat_axis=0, tiled=True),
        lax.all_to_all(out_grad, "kvh", split_axis=1, concat_axis=0, tiled=True),
    )
    row_count = query_row_slice.shape[0]
    kv_local = key_row_slice.shape[1] // HEAD_SIZE
    group_width = query_row_slice.shape[1] // key_row_slice.shape[1]
    reach = (WINDOW_TOKENS + row_count - 1) // row_count
    shard_index = lax.axis_index("seq")
    row_offsets = jnp.arange(row_count, dtype=jnp.int32)
    query_pos = shard_index * row_count + row_offsets
    lower_key = jnp.maximum(file_start, query_pos - WINDOW_TOKENS + 1)
    paired = jnp.stack([key_row_slice, value_rows])
    window_blocks = [paired for block_index in range(reach + 1)]
    carried = paired
    for hop_count in range(1, reach + 1):
        carried = shifted(carried, "seq", 1)
        window_blocks[reach - hop_count] = carried
    key_positions = [
        (shard_index - reach + block_index) * row_count + row_offsets
        for block_index in range(reach + 1)
    ]
    shaped_queries = query_row_slice.reshape(row_count, kv_local, group_width, HEAD_SIZE)
    shaped_grads = grad_rows.reshape(row_count, kv_local, group_width, HEAD_SIZE)
    attention_parts = []
    query_parts = []
    total_parts = []
    delta_parts = []
    head_keys = []
    head_values = []
    for head_index in range(kv_local):
        low_col = head_index * HEAD_SIZE
        key_blocks = [
            block_pair[0][:, low_col : low_col + HEAD_SIZE] for block_pair in window_blocks
        ]
        value_blocks = [
            block_pair[1][:, low_col : low_col + HEAD_SIZE] for block_pair in window_blocks
        ]
        attn_low, query_grad, log_total, row_delta, key_grads, value_grads = head_pass(
            shaped_queries[:, head_index],
            shaped_grads[:, head_index],
            key_blocks,
            value_blocks,
            key_positions,
            query_pos,
            lower_key,
        )
        attention_parts.append(attn_low)
        query_parts.append(query_grad)
        total_parts.append(log_total)
        delta_parts.append(row_delta)
        head_keys.append(key_grads)
        head_values.append(value_grads)
    attention_all = jnp.stack(attention_parts, axis=1).reshape(
        row_count, kv_local * group_width * HEAD_SIZE
    )
    attention_back = lax.all_to_all(attention_all, "kvh", split_axis=0, concat_axis=1, tiled=True)
    own_grads = jnp.stack(
        [
            jnp.concatenate([head_keys[head_index][-1] for head_index in range(kv_local)], axis=1),
            jnp.concatenate(
                [head_values[head_index][-1] for head_index in range(kv_local)], axis=1
            ),
        ]
    )
    for hop_count in range(1, reach + 1):
        source_block = reach - hop_count
        partial_grads = jnp.stack(
            [
                jnp.concatenate(
                    [head_keys[head_index][source_block] for head_index in range(kv_local)], axis=1
                ),
                jnp.concatenate(
                    [head_values[head_index][source_block] for head_index in range(kv_local)],
                    axis=1,
                ),
            ]
        )
        own_grads = own_grads + shifted(partial_grads, "seq", -hop_count)
    query_all = jnp.stack(query_parts, axis=1).reshape(
        row_count, kv_local * group_width * HEAD_SIZE
    )
    grads_low = own_grads.astype(jnp.bfloat16)
    query_back, key_back, value_back = (
        lax.all_to_all(query_all, "kvh", split_axis=0, concat_axis=1, tiled=True),
        lax.all_to_all(grads_low[0], "kvh", split_axis=0, concat_axis=1, tiled=True),
        lax.all_to_all(grads_low[1], "kvh", split_axis=0, concat_axis=1, tiled=True),
    )
    return (attention_back, query_back, key_back, value_back)


def solution(mesh):
    in_specs = (
        P(("seq", "kvh"), None),
        P(("seq", "kvh"), None),
        P(("seq", "kvh"), None),
        P(("seq", "kvh"), None),
        P("seq"),
    )
    out_specs = (
        P(("seq", "kvh"), None),
        P(("seq", "kvh"), None),
        P(("seq", "kvh"), None),
        P(("seq", "kvh"), None),
    )
    return jax.shard_map(body, mesh=mesh, in_specs=in_specs, out_specs=out_specs, check_vma=False)
```

profile of v0, /device:TPU:4, one launch (start us, length us, event | category | flops | bytes accessed | tf_op | source)
XLA Modules:
  0.0 302.2 jit_solution(15509098615407994288)
XLA Ops:
  0.7 1.8 copy.1032
  2.4 3.4 %all-to-all-start = ((bf16[64,4,512]{2,0,1:T(8,128)(2,1)}), bf16[64,4,512]{2,0,1:T(8,128)(2,1)S(1)}, u32[]{:S(2)}, u32[]{:S(2)}) async-start(bf16[64,4,512]{2,0,1:T(8,128)(2,1)} %bitcast.993), calls=%async_computation | async-start | bytes 524288 | tf_op jit(solution)/shard_map/all_to_all | solution.py:91
  5.8 1.0 copy.1031
  6.8 5.0 %all-to-all-done = bf16[64,4,512]{2,0,1:T(8,128)(2,1)S(1)} async-done(((bf16[64,4,512]{2,0,1:T(8,128)(2,1)}), bf16[64,4,512]{2,0,1:T(8,128)(2,1)S(1)}, u32[]{:S(2)}, u32[]{:S(2)}) %all-to-all-start) | async-done | bytes 262176 | tf_op jit(solution)/shard_map/all_to_all | solution.py:91
  11.8 8.4 %all_to_all.146 = bf16[64,4,512]{2,0,1:T(8,128)(2,1)S(1)} all-to-all(bf16[64,4,512]{2,0,1:T(8,128)(2,1)S(1)} %bitcast.1018), channel_id=1, replica_groups=mesh['seq'=8,'kvh'=4] {'kvh'}, dimensions={1} | all-to-all | bytes 524288 | tf_op jit(solution)/shard_map/all_to_all | solution.py:92
  20.3 3.4 %collective-permute-start = (bf16[2,256,512]{2,1,0:T(8,128)(2,1)S(1)}, bf16[2,256,512]{2,1,0:T(8,128)(2,1)S(1)}, u32[]{:S(2)}, u32[]{:S(2)}) collective-permute-start(bf16[2,256,512]{2,1,0:T(8,128)(2,1)S(1)} %pad_maximum_fusion.4), channel_id=1, source_target_pairs={{0,4},{4,8},{8,12},{12,16},{16,20},{20,24},{24,28},{1,5},{5,9},{9,... | collective-permute-start | bytes 1572872 | tf_op jit(solution)/shard_map/ppermute | solution.py:16
  24.6 3.5 %all-to-all-start.2 = ((bf16[64,4,1024]{2,0,1:T(8,128)(2,1)}), bf16[64,4,1024]{2,0,1:T(8,128)(2,1)S(1)}, u32[]{:S(2)}, u32[]{:S(2)}) async-start(bf16[64,4,1024]{2,0,1:T(8,128)(2,1)} %bitcast.991), calls=%async_computation.2 | async-start | bytes 1048576 | tf_op jit(solution)/shard_map/all_to_all | solution.py:90
  28.1 7.4 %collective-permute-done = bf16[2,256,512]{2,1,0:T(8,128)(2,1)S(1)} collective-permute-done((bf16[2,256,512]{2,1,0:T(8,128)(2,1)S(1)}, bf16[2,256,512]{2,1,0:T(8,128)(2,1)S(1)}, u32[]{:S(2)}, u32[]{:S(2)}) %collective-permute-start) | collective-permute-done | bytes 524320 | tf_op jit(solution)/shard_map/ppermute | solution.py:16
  35.5 4.3 %collective-permute-start.1 = (bf16[2,256,512]{2,1,0:T(8,128)(2,1)S(1)}, bf16[2,256,512]{2,1,0:T(8,128)(2,1)}, u32[]{:S(2)}, u32[]{:S(2)}) collective-permute-start(bf16[2,256,512]{2,1,0:T(8,128)(2,1)S(1)} %collective-permute-done), channel_id=1, source_target_pairs={{0,4},{4,8},{8,12},{12,16},{16,20},{20,24},{24,28},{1,5},{5,9},{9,... | collective-permute-start | bytes 1572872 | tf_op jit(solution)/shard_map/ppermute | solution.py:16
  40.7 3.5 %all-to-all-start.4 = ((bf16[64,4,1024]{2,0,1:T(8,128)(2,1)}), bf16[64,4,1024]{2,0,1:T(8,128)(2,1)S(1)}, u32[]{:S(2)}, u32[]{:S(2)}) async-start(bf16[64,4,1024]{2,0,1:T(8,128)(2,1)} %bitcast.990), calls=%async_computation.4 | async-start | bytes 1048576 | tf_op jit(solution)/shard_map/all_to_all | solution.py:93
  44.2 5.7 %collective-permute-done.1 = bf16[2,256,512]{2,1,0:T(8,128)(2,1)} collective-permute-done((bf16[2,256,512]{2,1,0:T(8,128)(2,1)S(1)}, bf16[2,256,512]{2,1,0:T(8,128)(2,1)}, u32[]{:S(2)}, u32[]{:S(2)}) %collective-permute-start.1) | collective-permute-done | bytes 524320 | tf_op jit(solution)/shard_map/ppermute | solution.py:16
  49.9 5.2 %collective-permute-start.2 = (bf16[2,256,512]{2,1,0:T(8,128)(2,1)}, bf16[2,256,512]{2,1,0:T(8,128)(2,1)}, u32[]{:S(2)}, u32[]{:S(2)}) collective-permute-start(bf16[2,256,512]{2,1,0:T(8,128)(2,1)} %collective-permute-done.1), channel_id=1, source_target_pairs={{0,4},{4,8},{8,12},{12,16},{16,20},{20,24},{24,28},{1,5},{5,9},{9,... | collective-permute-start | bytes 1572872 | tf_op jit(solution)/shard_map/ppermute | solution.py:16
  55.1 0.9 compare_and_fusion
  58.0 6.4 %collective-permute-done.2 = bf16[2,256,512]{2,1,0:T(8,128)(2,1)} collective-permute-done((bf16[2,256,512]{2,1,0:T(8,128)(2,1)}, bf16[2,256,512]{2,1,0:T(8,128)(2,1)}, u32[]{:S(2)}, u32[]{:S(2)}) %collective-permute-start.2) | collective-permute-done | bytes 524320 | tf_op jit(solution)/shard_map/ppermute | solution.py:16
  64.3 5.5 %collective-permute-start.3 = (bf16[2,256,512]{2,1,0:T(8,128)(2,1)}, bf16[2,256,512]{2,1,0:T(8,128)(2,1)S(1)}, u32[]{:S(2)}, u32[]{:S(2)}) collective-permute-start(bf16[2,256,512]{2,1,0:T(8,128)(2,1)} %collective-permute-done.2), channel_id=1, source_target_pairs={{0,4},{4,8},{8,12},{12,16},{16,20},{20,24},{24,28},{1,5},{5,9},{9,... | collective-permute-start | bytes 1572872 | tf_op jit(solution)/shard_map/ppermute | solution.py:16
  69.8 1.1 slice_bitcast_fusion.1
  70.9 1.1 slice_bitcast_fusion.2
  72.0 6.0 %collective-permute-done.3 = bf16[2,256,512]{2,1,0:T(8,128)(2,1)S(1)} collective-permute-done((bf16[2,256,512]{2,1,0:T(8,128)(2,1)}, bf16[2,256,512]{2,1,0:T(8,128)(2,1)S(1)}, u32[]{:S(2)}, u32[]{:S(2)}) %collective-permute-start.3) | collective-permute-done | bytes 524320 | tf_op jit(solution)/shard_map/ppermute | solution.py:16
  82.9 0.9 convolution_bitcast_fusion.56
  85.0 0.9 fusion.151
  89.9 0.9 convolution_bitcast_fusion.33
  90.8 0.9 convolution_bitcast_fusion.41
  94.1 0.9 fusion.150
  98.0 0.9 convolution_bitcast_fusion.26
  107.0 0.9 convolution_bitcast_fusion.27
  109.9 0.9 convolution_bitcast_fusion.59
  113.4 0.9 fusion.148
  114.3 0.9 fusion.147
  115.4 0.9 fusion.155
  116.9 0.9 fusion.139
  117.8 0.9 fusion.132
  119.8 0.9 fusion.154
  121.1 0.9 fusion.107
  122.0 0.9 fusion.145
  122.9 0.9 fusion.141
  123.8 0.9 fusion.153
  125.1 0.9 fusion.111
  127.1 0.9 fusion.144
  128.2 0.9 fusion.140
  129.1 0.9 fusion.115
  130.6 1.2 all_to_all.119
  131.7 3.6 %all-to-all-start.3 = ((bf16[4,64,1024]{2,1,0:T(8,128)(2,1)}), bf16[4,64,1024]{2,1,0:T(8,128)(2,1)S(1)}, u32[]{:S(2)}, u32[]{:S(2)}) async-start(bf16[4,64,1024]{2,1,0:T(8,128)(2,1)} %all_to_all.119), calls=%async_computation.3 | async-start | bytes 1048576 | tf_op jit(solution)/shard_map/all_to_all | solution.py:147
  135.5 1.1 maximum_bitcast_fusion.2
  136.7 2.1 collective-permute-start.4
  139.0 1.0 pad_maximum_fusion.1
  140.1 1.4 collective-permute-start.5
  141.7 1.0 pad_maximum_fusion.3
  142.7 1.4 collective-permute-start.7
  144.3 1.1 pad_maximum_fusion.2
  145.4 1.4 collective-permute-start.6
  147.6 0.9 fusion.138
  148.5 0.9 fusion.137
  150.0 1.2 all_to_all.126
  151.4 1.1 maximum_bitcast_fusion
  152.5 3.5 %all-to-all-start.5 = ((bf16[4,64,1024]{2,1,0:T(8,128)(2,1)}), bf16[4,64,1024]{2,1,0:T(8,128)(2,1)S(1)}, u32[]{:S(2)}, u32[]{:S(2)}) async-start(bf16[4,64,1024]{2,1,0:T(8,128)(2,1)} %all_to_all.126), calls=%async_computation.5 | async-start | bytes 1048576 | tf_op jit(solution)/shard_map/all_to_all | solution.py:175
  156.0 10.2 %collective-permute-done.4 = f32[2,256,512]{1,2,0:T(8,128)} collective-permute-done((f32[2,256,512]{1,2,0:T(8,128)S(1)}, f32[2,256,512]{1,2,0:T(8,128)}, u32[]{:S(2)}, u32[]{:S(2)}) %collective-permute-start.4) | collective-permute-done | bytes 1048608 | tf_op jit(solution)/shard_map/ppermute | solution.py:16
  166.2 4.0 %collective-permute-done.5 = f32[2,256,512]{1,2,0:T(8,128)} collective-permute-done((f32[2,256,512]{1,2,0:T(8,128)}, f32[2,256,512]{1,2,0:T(8,128)}, u32[]{:S(2)}, u32[]{:S(2)}) %collective-permute-start.5) | collective-permute-done | bytes 1048608 | tf_op jit(solution)/shard_map/ppermute | solution.py:16
  170.2 46.4 %collective-permute-done.7 = f32[2,256,512]{1,2,0:T(8,128)} collective-permute-done((f32[2,256,512]{1,2,0:T(8,128)}, f32[2,256,512]{1,2,0:T(8,128)}, u32[]{:S(2)}, u32[]{:S(2)}) %collective-permute-start.7) | collective-permute-done | bytes 1048608 | tf_op jit(solution)/shard_map/ppermute | solution.py:16
  216.6 62.7 %collective-permute-done.6 = f32[2,256,512]{1,2,0:T(8,128)} collective-permute-done((f32[2,256,512]{1,2,0:T(8,128)}, f32[2,256,512]{1,2,0:T(8,128)}, u32[]{:S(2)}, u32[]{:S(2)}) %collective-permute-start.6) | collective-permute-done | bytes 1048608 | tf_op jit(solution)/shard_map/ppermute | solution.py:16
  279.3 2.4 fusion.159
  282.7 3.4 %all-to-all-start.7 = ((bf16[4,64,512]{2,1,0:T(8,128)(2,1)}), bf16[4,64,512]{2,1,0:T(8,128)(2,1)S(1)}, u32[]{:S(2)}, u32[]{:S(2)}) async-start(bf16[4,64,512]{2,1,0:T(8,128)(2,1)} %bitcast.224), calls=%async_computation.7 | async-start | bytes 524288 | tf_op jit(solution)/shard_map/all_to_all | solution.py:177
  286.9 5.2 %all-to-all-done.7 = bf16[4,64,512]{2,1,0:T(8,128)(2,1)S(1)} async-done(((bf16[4,64,512]{2,1,0:T(8,128)(2,1)}), bf16[4,64,512]{2,1,0:T(8,128)(2,1)S(1)}, u32[]{:S(2)}, u32[]{:S(2)}) %all-to-all-start.7) | async-done | bytes 262176 | tf_op jit(solution)/shard_map/all_to_all | solution.py:177
  292.1 3.4 %all-to-all-start.6 = ((bf16[4,64,512]{2,1,0:T(8,128)(2,1)}), bf16[4,64,512]{2,1,0:T(8,128)(2,1)S(1)}, u32[]{:S(2)}, u32[]{:S(2)}) async-start(bf16[4,64,512]{2,1,0:T(8,128)(2,1)} %bitcast.222), calls=%async_computation.6 | async-start | bytes 524288 | tf_op jit(solution)/shard_map/all_to_all | solution.py:176
  297.9 3.6 %all-to-all-done.6 = bf16[4,64,512]{2,1,0:T(8,128)(2,1)S(1)} async-done(((bf16[4,64,512]{2,1,0:T(8,128)(2,1)}), bf16[4,64,512]{2,1,0:T(8,128)(2,1)S(1)}, u32[]{:S(2)}, u32[]{:S(2)}) %all-to-all-start.6) | async-done | bytes 262176 | tf_op jit(solution)/shard_map/all_to_all | solution.py:176
  (224 shorter events, 43.0 us)
Async XLA Ops:
  0.6 23.1 %copy-start.3 = (bf16[64,4096]{1,0:T(8,128)(2,1)S(1)}, bf16[64,4096]{1,0:T(8,128)(2,1)}, u32[]{:S(2)}) copy-start(bf16[64,4096]{1,0:T(8,128)(2,1)} %param.5) | copy-start | bytes 1572868
  0.6 39.2 %copy-start.4 = (bf16[64,4096]{1,0:T(8,128)(2,1)S(1)}, bf16[64,4096]{1,0:T(8,128)(2,1)}, u32[]{:S(2)}) copy-start(bf16[64,4096]{1,0:T(8,128)(2,1)} %param.8) | copy-start | bytes 1572868
  2.4 9.4 %all-to-all-start = ((bf16[64,4,512]{2,0,1:T(8,128)(2,1)}), bf16[64,4,512]{2,0,1:T(8,128)(2,1)S(1)}, u32[]{:S(2)}, u32[]{:S(2)}) async-start(bf16[64,4,512]{2,0,1:T(8,128)(2,1)} %bitcast.993), calls=%async_computation | async-start | bytes 524288 | tf_op jit(solution)/shard_map/all_to_all | solution.py:91
  5.8 34.8 %copy-start.35 = (s32[256]{0:T(256)S(1)}, s32[256]{0:T(256)}, u32[]{:S(2)}) copy-start(s32[256]{0:T(256)} %param.9) | copy-start | bytes 3076
  20.3 15.2 %collective-permute-start = (bf16[2,256,512]{2,1,0:T(8,128)(2,1)S(1)}, bf16[2,256,512]{2,1,0:T(8,128)(2,1)S(1)}, u32[]{:S(2)}, u32[]{:S(2)}) collective-permute-start(bf16[2,256,512]{2,1,0:T(8,128)(2,1)S(1)} %pad_maximum_fusion.4), channel_id=1, source_target_pairs={{0,4},{4,8},{8,12},{12,16},{16,20},{20,24},{24,28},{1,5},{5,9},{9,... | collective-permute-start | bytes 1572872 | tf_op jit(solution)/shard_map/ppermute | solution.py:16
  24.6 16.1 %all-to-all-start.2 = ((bf16[64,4,1024]{2,0,1:T(8,128)(2,1)}), bf16[64,4,1024]{2,0,1:T(8,128)(2,1)S(1)}, u32[]{:S(2)}, u32[]{:S(2)}) async-start(bf16[64,4,1024]{2,0,1:T(8,128)(2,1)} %bitcast.991), calls=%async_computation.2 | async-start | bytes 1048576 | tf_op jit(solution)/shard_map/all_to_all | solution.py:90
  35.5 14.4 %collective-permute-start.1 = (bf16[2,256,512]{2,1,0:T(8,128)(2,1)S(1)}, bf16[2,256,512]{2,1,0:T(8,128)(2,1)}, u32[]{:S(2)}, u32[]{:S(2)}) collective-permute-start(bf16[2,256,512]{2,1,0:T(8,128)(2,1)S(1)} %collective-permute-done), channel_id=1, source_target_pairs={{0,4},{4,8},{8,12},{12,16},{16,20},{20,24},{24,28},{1,5},{5,9},{9,... | collective-permute-start | bytes 1572872 | tf_op jit(solution)/shard_map/ppermute | solution.py:16
  40.7 15.7 %all-to-all-start.4 = ((bf16[64,4,1024]{2,0,1:T(8,128)(2,1)}), bf16[64,4,1024]{2,0,1:T(8,128)(2,1)S(1)}, u32[]{:S(2)}, u32[]{:S(2)}) async-start(bf16[64,4,1024]{2,0,1:T(8,128)(2,1)} %bitcast.990), calls=%async_computation.4 | async-start | bytes 1048576 | tf_op jit(solution)/shard_map/all_to_all | solution.py:93
  49.9 14.5 %collective-permute-start.2 = (bf16[2,256,512]{2,1,0:T(8,128)(2,1)}, bf16[2,256,512]{2,1,0:T(8,128)(2,1)}, u32[]{:S(2)}, u32[]{:S(2)}) collective-permute-start(bf16[2,256,512]{2,1,0:T(8,128)(2,1)} %collective-permute-done.1), channel_id=1, source_target_pairs={{0,4},{4,8},{8,12},{12,16},{16,20},{20,24},{24,28},{1,5},{5,9},{9,... | collective-permute-start | bytes 1572872 | tf_op jit(solution)/shard_map/ppermute | solution.py:16
  57.6 20.4 %copy-start.34 = (pred[256,256]{0,1:T(8,128)(4,1)S(1)}, pred[256,256]{0,1:T(8,128)(4,1)}, u32[]{:S(2)}) copy-start(pred[256,256]{0,1:T(8,128)(4,1)} %get-tuple-element.73) | copy-start | bytes 196612
  64.3 13.6 %collective-permute-start.3 = (bf16[2,256,512]{2,1,0:T(8,128)(2,1)}, bf16[2,256,512]{2,1,0:T(8,128)(2,1)S(1)}, u32[]{:S(2)}, u32[]{:S(2)}) collective-permute-start(bf16[2,256,512]{2,1,0:T(8,128)(2,1)} %collective-permute-done.2), channel_id=1, source_target_pairs={{0,4},{4,8},{8,12},{12,16},{16,20},{20,24},{24,28},{1,5},{5,9},{9,... | collective-permute-start | bytes 1572872 | tf_op jit(solution)/shard_map/ppermute | solution.py:16
  131.7 7.1 %copy-start.9 = (f32[256,128]{0,1:T(8,128)S(1)}, f32[256,128]{0,1:T(8,128)}, u32[]{:S(2)}) copy-start(f32[256,128]{0,1:T(8,128)} %convolution_bitcast_fusion.40) | copy-start | bytes 393220
  131.7 7.1 %copy-start.14 = (f32[256,128]{0,1:T(8,128)S(1)}, f32[256,128]{0,1:T(8,128)}, u32[]{:S(2)}) copy-start(f32[256,128]{0,1:T(8,128)} %convolution_bitcast_fusion.41) | copy-start | bytes 393220
  131.7 7.1 %copy-start.19 = (f32[256,128]{0,1:T(8,128)S(1)}, f32[256,128]{0,1:T(8,128)}, u32[]{:S(2)}) copy-start(f32[256,128]{0,1:T(8,128)} %convolution_bitcast_fusion.42) | copy-start | bytes 393220
  131.7 20.7 %all-to-all-start.3 = ((bf16[4,64,1024]{2,1,0:T(8,128)(2,1)}), bf16[4,64,1024]{2,1,0:T(8,128)(2,1)S(1)}, u32[]{:S(2)}, u32[]{:S(2)}) async-start(bf16[4,64,1024]{2,1,0:T(8,128)(2,1)} %all_to_all.119), calls=%async_computation.3 | async-start | bytes 1048576 | tf_op jit(solution)/shard_map/all_to_all | solution.py:147
  135.4 3.4 %copy-start.25 = (f32[256,128]{0,1:T(8,128)S(1)}, f32[256,128]{0,1:T(8,128)}, u32[]{:S(2)}) copy-start(f32[256,128]{0,1:T(8,128)} %convolution_bitcast_fusion.43) | copy-start | bytes 393220
  135.4 3.5 %copy-start.27 = (f32[256,128]{0,1:T(8,128)S(1)}, f32[256,128]{0,1:T(8,128)}, u32[]{:S(2)}) copy-start(f32[256,128]{0,1:T(8,128)} %fusion.147) | copy-start | bytes 393220
  135.4 3.5 %copy-start.30 = (f32[256,128]{0,1:T(8,128)S(1)}, f32[256,128]{0,1:T(8,128)}, u32[]{:S(2)}) copy-start(f32[256,128]{0,1:T(8,128)} %fusion.146) | copy-start | bytes 393220
  135.4 3.5 %copy-start.32 = (f32[256,128]{0,1:T(8,128)S(1)}, f32[256,128]{0,1:T(8,128)}, u32[]{:S(2)}) copy-start(f32[256,128]{0,1:T(8,128)} %fusion.145) | copy-start | bytes 393220
  135.4 3.5 %copy-start.33 = (f32[256,128]{0,1:T(8,128)S(1)}, f32[256,128]{0,1:T(8,128)}, u32[]{:S(2)}) copy-start(f32[256,128]{0,1:T(8,128)} %fusion.144) | copy-start | bytes 393220
  136.7 4.8 %copy-start.7 = (f32[256,128]{0,1:T(8,128)S(1)}, f32[256,128]{0,1:T(8,128)}, u32[]{:S(2)}) copy-start(f32[256,128]{0,1:T(8,128)} %convolution_bitcast_fusion.24) | copy-start | bytes 393220
  136.7 4.8 %copy-start.13 = (f32[256,128]{0,1:T(8,128)S(1)}, f32[256,128]{0,1:T(8,128)}, u32[]{:S(2)}) copy-start(f32[256,128]{0,1:T(8,128)} %convolution_bitcast_fusion.25) | copy-start | bytes 393220
  136.7 4.8 %copy-start.18 = (f32[256,128]{0,1:T(8,128)S(1)}, f32[256,128]{0,1:T(8,128)}, u32[]{:S(2)}) copy-start(f32[256,128]{0,1:T(8,128)} %convolution_bitcast_fusion.26) | copy-start | bytes 393220
  136.7 4.8 %copy-start.22 = (f32[256,128]{0,1:T(8,128)S(1)}, f32[256,128]{0,1:T(8,128)}, u32[]{:S(2)}) copy-start(f32[256,128]{0,1:T(8,128)} %convolution_bitcast_fusion.27) | copy-start | bytes 393220
  136.7 4.9 %copy-start.26 = (f32[256,128]{0,1:T(8,128)S(1)}, f32[256,128]{0,1:T(8,128)}, u32[]{:S(2)}) copy-start(f32[256,128]{0,1:T(8,128)} %fusion.155) | copy-start | bytes 393220
  136.7 4.9 %copy-start.28 = (f32[256,128]{0,1:T(8,128)S(1)}, f32[256,128]{0,1:T(8,128)}, u32[]{:S(2)}) copy-start(f32[256,128]{0,1:T(8,128)} %fusion.154) | copy-start | bytes 393220
  136.7 4.9 %copy-start.29 = (f32[256,128]{0,1:T(8,128)S(1)}, f32[256,128]{0,1:T(8,128)}, u32[]{:S(2)}) copy-start(f32[256,128]{0,1:T(8,128)} %fusion.153) | copy-start | bytes 393220
  136.7 4.9 %copy-start.31 = (f32[256,128]{0,1:T(8,128)S(1)}, f32[256,128]{0,1:T(8,128)}, u32[]{:S(2)}) copy-start(f32[256,128]{0,1:T(8,128)} %fusion.152) | copy-start | bytes 393220
  136.7 29.4 %collective-permute-start.4 = (f32[2,256,512]{1,2,0:T(8,128)S(1)}, f32[2,256,512]{1,2,0:T(8,128)}, u32[]{:S(2)}, u32[]{:S(2)}) collective-permute-start(f32[2,256,512]{1,2,0:T(8,128)S(1)} %pad_maximum_fusion), channel_id=1, source_target_pairs={{4,0},{8,4},{12,8},{16,12},{20,16},{24,20},{28,24},{5,1},{9,5},{13... | collective-permute-start | bytes 3145736 | tf_op jit(solution)/shard_map/ppermute | solution.py:16
  140.0 4.1 %copy-start.6 = (f32[256,128]{0,1:T(8,128)S(1)}, f32[256,128]{0,1:T(8,128)}, u32[]{:S(2)}) copy-start(f32[256,128]{0,1:T(8,128)} %convolution_bitcast_fusion.32) | copy-start | bytes 393220
  140.0 4.1 %copy-start.11 = (f32[256,128]{0,1:T(8,128)S(1)}, f32[256,128]{0,1:T(8,128)}, u32[]{:S(2)}) copy-start(f32[256,128]{0,1:T(8,128)} %convolution_bitcast_fusion.33) | copy-start | bytes 393220
  140.0 4.1 %copy-start.16 = (f32[256,128]{0,1:T(8,128)S(1)}, f32[256,128]{0,1:T(8,128)}, u32[]{:S(2)}) copy-start(f32[256,128]{0,1:T(8,128)} %convolution_bitcast_fusion.34) | copy-start | bytes 393220
  140.0 4.1 %copy-start.21 = (f32[256,128]{0,1:T(8,128)S(1)}, f32[256,128]{0,1:T(8,128)}, u32[]{:S(2)}) copy-start(f32[256,128]{0,1:T(8,128)} %convolution_bitcast_fusion.35) | copy-start | bytes 393220
  140.0 4.2 %copy-start.8 = (f32[256,128]{0,1:T(8,128)S(1)}, f32[256,128]{0,1:T(8,128)}, u32[]{:S(2)}) copy-start(f32[256,128]{0,1:T(8,128)} %fusion.151) | copy-start | bytes 393220
  140.0 4.2 %copy-start.12 = (f32[256,128]{0,1:T(8,128)S(1)}, f32[256,128]{0,1:T(8,128)}, u32[]{:S(2)}) copy-start(f32[256,128]{0,1:T(8,128)} %fusion.150) | copy-start | bytes 393220
  140.0 4.2 %copy-start.17 = (f32[256,128]{0,1:T(8,128)S(1)}, f32[256,128]{0,1:T(8,128)}, u32[]{:S(2)}) copy-start(f32[256,128]{0,1:T(8,128)} %fusion.149) | copy-start | bytes 393220
  140.1 4.2 %copy-start.24 = (f32[256,128]{0,1:T(8,128)S(1)}, f32[256,128]{0,1:T(8,128)}, u32[]{:S(2)}) copy-start(f32[256,128]{0,1:T(8,128)} %fusion.148) | copy-start | bytes 393220
  140.1 30.1 %collective-permute-start.5 = (f32[2,256,512]{1,2,0:T(8,128)}, f32[2,256,512]{1,2,0:T(8,128)}, u32[]{:S(2)}, u32[]{:S(2)}) collective-permute-start(f32[2,256,512]{1,2,0:T(8,128)} %pad_maximum_fusion.1), channel_id=1, source_target_pairs={{8,0},{12,4},{16,8},{20,12},{24,16},{28,20},{9,1},{13,5},{17,9},{2... | collective-permute-start | bytes 3145736 | tf_op jit(solution)/shard_map/ppermute | solution.py:16
  142.7 4.1 %copy-start = (f32[256,2,128]{0,2,1:T(8,128)S(1)}, f32[256,2,128]{0,2,1:T(8,128)}, u32[]{:S(2)}) copy-start(f32[256,2,128]{0,2,1:T(8,128)} %fusion.107) | copy-start | bytes 786436
  142.7 4.4 %copy-start.1 = (f32[256,2,128]{0,2,1:T(8,128)S(1)}, f32[256,2,128]{0,2,1:T(8,128)}, u32[]{:S(2)}) copy-start(f32[256,2,128]{0,2,1:T(8,128)} %fusion.111) | copy-start | bytes 786436
  142.7 4.6 %copy-start.2 = (f32[256,2,128]{0,2,1:T(8,128)S(1)}, f32[256,2,128]{0,2,1:T(8,128)}, u32[]{:S(2)}) copy-start(f32[256,2,128]{0,2,1:T(8,128)} %fusion.115) | copy-start | bytes 786436
  142.7 73.9 %collective-permute-start.7 = (f32[2,256,512]{1,2,0:T(8,128)}, f32[2,256,512]{1,2,0:T(8,128)}, u32[]{:S(2)}, u32[]{:S(2)}) collective-permute-start(f32[2,256,512]{1,2,0:T(8,128)} %pad_maximum_fusion.3), channel_id=1, source_target_pairs={{16,0},{20,4},{24,8},{28,12},{17,1},{21,5},{25,9},{29,13},{18,2},{... | collective-permute-start | bytes 3145736 | tf_op jit(solution)/shard_map/ppermute | solution.py:16
  144.2 3.3 %copy-start.5 = (f32[256,128]{0,1:T(8,128)S(1)}, f32[256,128]{0,1:T(8,128)}, u32[]{:S(2)}) copy-start(f32[256,128]{0,1:T(8,128)} %convolution_bitcast_fusion.56) | copy-start | bytes 393220
  144.3 3.3 %copy-start.10 = (f32[256,128]{0,1:T(8,128)S(1)}, f32[256,128]{0,1:T(8,128)}, u32[]{:S(2)}) copy-start(f32[256,128]{0,1:T(8,128)} %convolution_bitcast_fusion.57) | copy-start | bytes 393220
  144.3 3.3 %copy-start.15 = (f32[256,128]{0,1:T(8,128)S(1)}, f32[256,128]{0,1:T(8,128)}, u32[]{:S(2)}) copy-start(f32[256,128]{0,1:T(8,128)} %convolution_bitcast_fusion.58) | copy-start | bytes 393220
  144.3 3.3 %copy-start.20 = (f32[256,128]{0,1:T(8,128)S(1)}, f32[256,128]{0,1:T(8,128)}, u32[]{:S(2)}) copy-start(f32[256,128]{0,1:T(8,128)} %convolution_bitcast_fusion.59) | copy-start | bytes 393220
  145.4 4.0 %copy-start.23 = (bf16[256,1,2,128]{0,3,2,1:T(8,128)(2,1)S(1)}, bf16[256,1,2,128]{0,3,2,1:T(8,128)(2,1)}, u32[]{:S(2)}) copy-start(bf16[256,1,2,128]{0,3,2,1:T(8,128)(2,1)} %fusion.132) | copy-start | bytes 393220
  145.4 133.9 %collective-permute-start.6 = (f32[2,256,512]{1,2,0:T(8,128)}, f32[2,256,512]{1,2,0:T(8,128)}, u32[]{:S(2)}, u32[]{:S(2)}) collective-permute-start(f32[2,256,512]{1,2,0:T(8,128)} %pad_maximum_fusion.2), channel_id=1, source_target_pairs={{12,0},{16,4},{20,8},{24,12},{28,16},{13,1},{17,5},{21,9},{25,13},... | collective-permute-start | bytes 3145736 | tf_op jit(solution)/shard_map/ppermute | solution.py:16
  152.5 130.2 %all-to-all-start.5 = ((bf16[4,64,1024]{2,1,0:T(8,128)(2,1)}), bf16[4,64,1024]{2,1,0:T(8,128)(2,1)S(1)}, u32[]{:S(2)}, u32[]{:S(2)}) async-start(bf16[4,64,1024]{2,1,0:T(8,128)(2,1)} %all_to_all.126), calls=%async_computation.5 | async-start | bytes 1048576 | tf_op jit(solution)/shard_map/all_to_all | solution.py:175
  282.7 9.4 %all-to-all-start.7 = ((bf16[4,64,512]{2,1,0:T(8,128)(2,1)}), bf16[4,64,512]{2,1,0:T(8,128)(2,1)S(1)}, u32[]{:S(2)}, u32[]{:S(2)}) async-start(bf16[4,64,512]{2,1,0:T(8,128)(2,1)} %bitcast.224), calls=%async_computation.7 | async-start | bytes 524288 | tf_op jit(solution)/shard_map/all_to_all | solution.py:177
  292.1 9.4 %all-to-all-start.6 = ((bf16[4,64,512]{2,1,0:T(8,128)(2,1)}), bf16[4,64,512]{2,1,0:T(8,128)(2,1)S(1)}, u32[]{:S(2)}, u32[]{:S(2)}) async-start(bf16[4,64,512]{2,1,0:T(8,128)(2,1)} %bitcast.222), calls=%async_computation.6 | async-start | bytes 524288 | tf_op jit(solution)/shard_map/all_to_all | solution.py:176
where the time goes:
time: 303 us; the launch traced here: 302 us
  waiting for transfers between devices  163 us (54%)
  matrix products  51.2 us (17%)
  starting transfers between devices  49.1 us (16%)
  local copies, waits for them, and re-layouts  16.8 us (6%)
  other arithmetic  12.2 us (4%)
  blocking collectives  8.41 us (3%)
    ppermute x8, waiting for transfers between devices, shifted(): lax.ppermute(value, axis, [(source, source + steps) for source in range(l...  149 us
    dot_general x100, matrix products, product(): jnp.einsum(einsum_form, left_side, right_side, preferred_element_type=jnp...  46.3 us
    ppermute x8, starting transfers between devices, shifted(): lax.ppermute(value, axis, [(source, source + steps) for source in range(l...  24.7 us
    all_to_all x1, blocking collectives, body(): lax.all_to_all(values, 'kvh', split_axis=1, concat_axis=0, tiled=True)  8.41 us
  transfers between devices with their start and end apart: 15, of which 11 were waited for; matrix products, arithmetic and copies ran while one was open for 8% of the time, Pallas kernels for 0%

commit v1 on v0

v1 whole, which is shorter than its diff:
```python
import functools
import math

import jax
import jax.numpy as jnp
from jax import lax
from jax.experimental import pallas as pl
from jax.experimental.pallas import tpu as pltpu
from jax.sharding import PartitionSpec as P

HEAD_SIZE = 128
WINDOW_TOKENS = 1024
SCALE = 168.0 ** (-0.5)
EXP2_SCALE = SCALE / math.log(2.0)
MASKED = -1e30
MESH = pl.DeviceIdType.MESH

NT = (((1,), (1,)), ((), ()))
NN = (((1,), (0,)), ((), ()))
TN = (((0,), (0,)), ((), ()))


def matmul(left, right, dims):
    return lax.dot_general(left, right, dims, preferred_element_type=jnp.float32)


def kernel(
    seq_count, kvh_count, kv_local, group, rows, reach,
    q_in, k_in, v_in, g_in, starts_ref,
    attn_out, dq_out, dk_out, dv_out,
    kv, qg, scores, out_t, dq_t, attn_buf, dq_buf, part, pair_send, pair_recv,
    chain_send, chain_recv, dkv_low,
    in_send, in_recv, in_local, out_send, out_recv, out_local,
    hop_send, mate_send, window_recv, back_pair_send, back_pair_recv,
    back_chain_send, back_chain_recv,
):
    depth = reach + reach % 2
    seq = lax.axis_index("seq")
    me = lax.axis_index("kvh")
    odd = lax.rem(seq, 2)
    mate = seq + 1 - 2 * odd
    piece = rows // kvh_count
    width = group * HEAD_SIZE
    has_next = seq + 2 < seq_count
    has_previous = seq >= 2

    barrier = pltpu.get_barrier_semaphore()
    for off in range(1, kvh_count):
        pl.semaphore_signal(
            barrier, inc=1, device_id=(seq, lax.rem(me + off, kvh_count)), device_id_type=MESH
        )
    pl.semaphore_signal(barrier, inc=1, device_id=(mate, me), device_id_type=MESH)

    @pl.when(has_next)
    def _():
        pl.semaphore_signal(barrier, inc=1, device_id=(seq + 2, me), device_id_type=MESH)

    @pl.when(has_previous)
    def _():
        pl.semaphore_signal(barrier, inc=1, device_id=(seq - 2, me), device_id_type=MESH)

    pl.semaphore_wait(
        barrier, kvh_count + has_next.astype(jnp.int32) + has_previous.astype(jnp.int32)
    )

    sources = (k_in, v_in, q_in, g_in)
    widths = (HEAD_SIZE, HEAD_SIZE, width, width)
    targets = (attn_out, dq_out, dk_out, dv_out)
    out_widths = (width, width, HEAD_SIZE, HEAD_SIZE)

    def in_source(kind, head, owner):
        start = pl.multiple_of((owner * kv_local + head) * widths[kind], 128)
        return sources[kind].at[:, pl.ds(start, widths[kind])]

    def in_target(kind, head):
        block = pl.ds(pl.multiple_of(me * piece, piece), piece)
        if kind < 2:
            return kv.at[0, head, kind, block, :]
        return qg.at[head, kind - 2, block, :]

    def in_copy(kind, head, off):
        peer = lax.rem(me + off, kvh_count)
        return pltpu.make_async_remote_copy(
            src_ref=in_source(kind, head, peer),
            dst_ref=in_target(kind, head),
            send_sem=in_send.at[kind, head, off - 1],
            recv_sem=in_recv.at[kind, head, off - 1],
            device_id=(seq, peer),
            device_id_type=MESH,
        )

    def in_own(kind, head):
        return pltpu.make_async_copy(
            in_source(kind, head, me), in_target(kind, head), in_local.at[kind, head]
        )

    def in_wait(kind, head):
        in_own(kind, head).wait()
        for off in range(1, kvh_count):
            in_copy(kind, head, off).wait_recv()

    def out_source(kind, head, owner):
        block = pl.ds(pl.multiple_of(owner * piece, piece), piece)
        if kind == 0:
            return attn_buf.at[head, block, :]
        if kind == 1:
            return dq_buf.at[head, block, :]
        return dkv_low.at[head, kind - 2, block, :]

    def out_target(kind, head):
        start = pl.multiple_of((me * kv_local + head) * out_widths[kind], 128)
        return targets[kind].at[:, pl.ds(start, out_widths[kind])]

    def out_copy(kind, head, off):
        peer = lax.rem(me + off, kvh_count)
        return pltpu.make_async_remote_copy(
            src_ref=out_source(kind, head, peer),
            dst_ref=out_target(kind, head),
            send_sem=out_send.at[kind, head, off - 1],
            recv_sem=out_recv.at[kind, head, off - 1],
            device_id=(seq, peer),
            device_id_type=MESH,
        )

    def out_own(kind, head):
        return pltpu.make_async_copy(
            out_source(kind, head, me), out_target(kind, head), out_local.at[kind, head]
        )

    def out_start(kind, head):
        for off in range(1, kvh_count):
            out_copy(kind, head, off).start()
        out_own(kind, head).start()

    def hop_copy(slot, head):
        return pltpu.make_async_remote_copy(
            src_ref=kv.at[slot, head],
            dst_ref=kv.at[slot + 2, head],
            send_sem=hop_send.at[slot // 2, head],
            recv_sem=window_recv.at[slot + 1, head],
            device_id=(seq + 2, me),
            device_id_type=MESH,
        )

    def mate_copy(slot, head):
        there = slot + 1 - 2 * odd
        return pltpu.make_async_remote_copy(
            src_ref=kv.at[slot, head],
            dst_ref=kv.at[there, head],
            send_sem=mate_send.at[slot // 2, head],
            recv_sem=window_recv.at[there - 1, head],
            device_id=(mate, me),
            device_id_type=MESH,
        )

    def arrived(slot, head):
        pltpu.make_async_remote_copy(
            src_ref=kv.at[slot, head],
            dst_ref=kv.at[slot, head],
            send_sem=hop_send.at[0, head],
            recv_sem=window_recv.at[slot - 1, head],
            device_id=(mate, me),
            device_id_type=MESH,
        ).wait_recv()

    def hops(slot):
        return jnp.logical_and(has_next, seq >= slot) if slot + 2 <= depth else None

    def mates(slot):
        if slot == 0:
            return odd == 0
        if slot + 1 <= reach:
            return seq >= slot
        return jnp.logical_and(odd == 1, seq >= slot)

    def send_on(slot, head):
        if hops(slot) is not None:
            @pl.when(hops(slot))
            def _():
                hop_copy(slot, head).start()

        @pl.when(mates(slot))
        def _():
            mate_copy(slot, head).start()

    def send_keys(head, carry):
        for kind in (0, 1):
            for off in range(1, kvh_count):
                in_copy(kind, head, off).start()
            in_own(kind, head).start()
        return carry

    def send_queries(head, carry):
        for kind in (2, 3):
            for off in range(1, kvh_count):
                in_copy(kind, head, off).start()
            in_own(kind, head).start()
        return carry

    lax.fori_loop(0, kv_local, send_keys, 0)
    lax.fori_loop(0, kv_local, send_queries, 0)

    def first_hop(head, carry):
        in_wait(0, head)
        in_wait(1, head)
        send_on(0, head)
        return carry

    lax.fori_loop(0, kv_local, first_hop, 0)

    for slot in range(2, depth, 2):

        def next_hop(head, carry, slot=slot):
            @pl.when(seq >= slot)
            def _():
                arrived(slot, head)

            send_on(slot, head)
            return carry

        lax.fori_loop(0, kv_local, next_hop, 0)

    row_pos = lax.broadcasted_iota(jnp.int32, (1, rows), 1)
    lower_row = jnp.maximum(starts_ref[...] - seq * rows, row_pos - (WINDOW_TOKENS - 1))
    lower = jnp.concatenate([lower_row] * group, axis=1)
    position = jnp.concatenate([row_pos] * group, axis=1)
    spots = lax.broadcasted_iota(jnp.int32, (rows, group * rows), 0)
    block_count = jnp.minimum(seq, reach) + 1

    def stacked(wide):
        return jnp.concatenate(
            [wide[:, i * HEAD_SIZE : (i + 1) * HEAD_SIZE] for i in range(group)], axis=0
        )

    def spread(tall):
        return jnp.concatenate([tall[i * rows : (i + 1) * rows] for i in range(group)], axis=1)

    def compute(head):
        queries = stacked(qg[head, 0])
        grads = stacked(qg[head, 1])

        def score_block(slot, peak):
            raw = matmul(kv[slot, head, 0], queries, NT)
            allowed = jnp.logical_and(
                spots >= lower + slot * rows, spots <= position + slot * rows
            )
            raw = jnp.where(allowed, raw, MASKED)
            scores[slot] = raw
            return jnp.maximum(peak, jnp.max(raw, axis=0, keepdims=True))

        peak = lax.fori_loop(
            0, block_count, score_block, jnp.full((1, group * rows), MASKED, jnp.float32)
        )
        out_t[...] = jnp.zeros_like(out_t)

        def value_block(slot, total):
            raised = jnp.exp2((scores[slot] - peak) * EXP2_SCALE)
            scores[slot] = raised
            out_t[...] += matmul(kv[slot, head, 1], raised.astype(jnp.bfloat16), TN)
            return total + jnp.sum(raised, axis=0, keepdims=True)

        total = lax.fori_loop(
            0, block_count, value_block, jnp.zeros((1, group * rows), jnp.float32)
        )
        inverse = 1.0 / total
        attention = (out_t[...] * inverse).astype(jnp.bfloat16).astype(jnp.float32)
        attn_buf[head] = spread(jnp.transpose(attention).astype(jnp.bfloat16))
        out_start(0, head)
        delta = jnp.sum(
            jnp.transpose(grads.astype(jnp.float32)) * attention, axis=0, keepdims=True
        )
        dq_t[...] = jnp.zeros_like(dq_t)

        def grad_block(slot):
            probs = scores[slot] * inverse
            value_part = matmul(probs.astype(jnp.bfloat16), grads, NN)
            prob_grad = matmul(kv[slot, head, 1], grads, NT)
            score_grad = (probs * (prob_grad - delta)).astype(jnp.bfloat16)
            key_part = matmul(score_grad, queries, NN) * SCALE
            dq_t[...] += matmul(kv[slot, head, 0], score_grad, TN)
            return key_part, value_part

        for slot in range(reach + 1):

            @pl.when(seq >= slot)
            def _(slot=slot):
                key_part, value_part = grad_block(slot)
                if slot % 2:
                    pair_send[slot // 2, head, 0] = key_part.astype(jnp.bfloat16)
                    pair_send[slot // 2, head, 1] = value_part.astype(jnp.bfloat16)
                    back_pair(slot, head).start()
                else:
                    part[slot // 2, head, 0] = key_part
                    part[slot // 2, head, 1] = value_part

        if depth > reach:
            part[depth // 2, head] = jnp.zeros_like(part[depth // 2, head])

        dq_buf[head] = spread(jnp.transpose(dq_t[...] * SCALE).astype(jnp.bfloat16))
        out_start(1, head)

    def back_pair(slot, head):
        there = slot // 2 + (1 - odd)
        return pltpu.make_async_remote_copy(
            src_ref=pair_send.at[slot // 2, head],
            dst_ref=pair_recv.at[there, head],
            send_sem=back_pair_send.at[slot // 2, head],
            recv_sem=back_pair_recv.at[there, head],
            device_id=(mate, me),
            device_id_type=MESH,
        )

    def back_chain(slot, head):
        return pltpu.make_async_remote_copy(
            src_ref=chain_send.at[slot // 2 - 1, head],
            dst_ref=chain_recv.at[slot // 2 - 1, head],
            send_sem=back_chain_send.at[slot // 2 - 1, head],
            recv_sem=back_chain_recv.at[slot // 2 - 1, head],
            device_id=(seq - 2, me),
            device_id_type=MESH,
        )

    def collect(slot, head):
        half = slot // 2

        @pl.when(mates(slot))
        def _():
            pltpu.make_async_remote_copy(
                src_ref=pair_recv.at[half, head],
                dst_ref=pair_recv.at[half, head],
                send_sem=back_pair_send.at[0, head],
                recv_sem=back_pair_recv.at[half, head],
                device_id=(mate, me),
                device_id_type=MESH,
            ).wait_recv()
            part[half, head] += pair_recv[half, head].astype(jnp.float32)

        if slot + 2 <= depth:

            @pl.when(hops(slot))
            def _():
                pltpu.make_async_remote_copy(
                    src_ref=chain_recv.at[half, head],
                    dst_ref=chain_recv.at[half, head],
                    send_sem=back_chain_send.at[half, head],
                    recv_sem=back_chain_recv.at[half, head],
                    device_id=(mate, me),
                    device_id_type=MESH,
                ).wait_recv()
                part[half, head] += chain_recv[half, head].astype(jnp.float32)

        if slot == 0:
            dkv_low[head] = part[0, head].astype(jnp.bfloat16)
            out_start(2, head)
            out_start(3, head)
        else:

            @pl.when(seq >= slot)
            def _():
                chain_send[half - 1, head] = part[half, head].astype(jnp.bfloat16)
                back_chain(slot, head).start()

    levels = depth // 2 + 1

    def step(turn, carry):
        @pl.when(turn < kv_local)
        def _():
            head = turn

            @pl.when(seq >= depth)
            def _():
                arrived(depth, head)

            send_on(depth, head)
            for slot in range(1, reach + 1, 2):

                @pl.when(seq >= slot)
                def _(slot=slot):
                    arrived(slot, head)

            in_wait(2, head)
            in_wait(3, head)
            compute(head)

        for level in range(levels):
            lag = level + 1

            @pl.when(jnp.logical_and(turn >= lag, turn < kv_local + lag))
            def _(level=level, lag=lag):
                collect(depth - 2 * level, turn - lag)

        return carry

    lax.fori_loop(0, kv_local + levels, step, 0)

    def finish(head, carry):
        for kind in range(4):
            out_own(kind, head).wait()
            for off in range(1, kvh_count):
                in_copy(kind, head, off).wait_send()
                out_copy(kind, head, off).wait()
        for slot in range(0, depth + 1, 2):
            if slot + 2 <= depth:

                @pl.when(hops(slot))
                def _(slot=slot):
                    hop_copy(slot, head).wait_send()

            @pl.when(mates(slot))
            def _(slot=slot):
                mate_copy(slot, head).wait_send()

            if slot > 0:

                @pl.when(seq >= slot)
                def _(slot=slot):
                    back_chain(slot, head).wait_send()

        for slot in range(1, reach + 1, 2):

            @pl.when(seq >= slot)
            def _(slot=slot):
                back_pair(slot, head).wait_send()

        return carry

    lax.fori_loop(0, kv_local, finish, 0)


def body(seq_count, kvh_count, queries, keys, values, out_grad, file_start):
    rows = file_start.shape[0]
    kv_local = keys.shape[1] // (HEAD_SIZE * kvh_count)
    group = queries.shape[1] // keys.shape[1]
    reach = (WINDOW_TOKENS + rows - 1) // rows
    depth = reach + reach % 2
    half = depth // 2
    bf16, f32 = jnp.bfloat16, jnp.float32
    block = (kv_local, 2, rows, HEAD_SIZE)
    width = group * HEAD_SIZE
    dma = pltpu.SemaphoreType.DMA
    vmem = pl.BlockSpec(memory_space=pltpu.VMEM)
    return pl.pallas_call(
        functools.partial(kernel, seq_count, kvh_count, kv_local, group, rows, reach),
        out_shape=tuple(
            jax.ShapeDtypeStruct(like.shape, bf16) for like in (queries, queries, keys, values)
        ),
        in_specs=[vmem] * 5,
        out_specs=(vmem,) * 4,
        scratch_shapes=[
            pltpu.VMEM((depth + 1, *block), bf16),
            pltpu.VMEM((kv_local, 2, rows, width), bf16),
            pltpu.VMEM((reach + 1, rows, group * rows), f32),
            pltpu.VMEM((HEAD_SIZE, group * rows), f32),
            pltpu.VMEM((HEAD_SIZE, group * rows), f32),
            pltpu.VMEM((kv_local, rows, width), bf16),
            pltpu.VMEM((kv_local, rows, width), bf16),
            pltpu.VMEM((half + 1, *block), f32),
            pltpu.VMEM((half, *block), bf16),
            pltpu.VMEM((half + 1, *block), bf16),
            pltpu.VMEM((half, *block), bf16),
            pltpu.VMEM((half, *block), bf16),
            pltpu.VMEM(block, bf16),
            dma((4, kv_local, kvh_count - 1)),
            dma((4, kv_local, kvh_count - 1)),
            dma((4, kv_local)),
            dma((4, kv_local, kvh_count - 1)),
            dma((4, kv_local, kvh_count - 1)),
            dma((4, kv_local)),
            dma((half, kv_local)),
            dma((half + 1, kv_local)),
            dma((depth, kv_local)),
            dma((half, kv_local)),
            dma((half + 1, kv_local)),
            dma((half, kv_local)),
            dma((half, kv_local)),
        ],
        compiler_params=pltpu.CompilerParams(
            collective_id=0, has_side_effects=True, vmem_limit_bytes=56 * 1024 * 1024
        ),
    )(queries, keys, values, out_grad, file_start.reshape(1, rows))


def solution(mesh):
    token_spec = P(("seq", "kvh"), None)
    return jax.shard_map(
        functools.partial(body, mesh.shape["seq"], mesh.shape["kvh"]),
        mesh=mesh,
        in_specs=(token_spec,) * 4 + (P("seq"),),
        out_specs=(token_spec,) * 4,
        check_vma=False,
    )
```

time: 303 us -> 89.4 us (0.30)
  the two profiles are of different devices: /device:TPU:4 before, /device:TPU:0 now
where the time goes in v1:
time: 89.4 us; the launch traced here: 89.2 us
  Pallas kernels  83.8 us (94%)
  local copies, waits for them, and re-layouts  4.77 us (5%)
    pallas_call x1, Pallas kernels, body(): pl.pallas_call(functools.partial(kernel, seq_count, kvh_count, kv_local,...  83.8 us
    unnamed x10, local copies, waits for them, and re-layouts  4.77 us

profile of v1, /device:TPU:0, one launch (start us, length us, event | category | flops | bytes accessed | tf_op | source)
XLA Modules:
  0.0 89.2 jit_solution(1282547383693568665)
XLA Ops:
  0.6 83.8 %shard_map.84 = (bf16[64,4096]{1,0:T(8,128)(2,1)}, bf16[64,4096]{1,0:T(8,128)(2,1)}, bf16[64,2048]{1,0:T(8,128)(2,1)}, bf16[64,2048]{1,0:T(8,128)(2,1)}) custom-call(bf16[64,4096]{1,0:T(8,128)(2,1)} %q_in.1, bf16[64,2048]{1,0:T(8,128)(2,1)} %k_in.1, bf16[64,2048]{1,0:T(8,128)(2,1)} %v_in.1, bf16[64,4096]{1,0:T(8,128)(2,1)} %g_in.1, s32[1,256]{1,0:T(1,128)} %bitcast.1), custom_call_target="tpu_custom_call" | custom-call | tf_op jit(solution)/shard_map/pallas_call | solution.py:442
  84.4 0.0 copy-start
  84.4 1.9 %copy.13 = bf16[64,4096]{1,0:T(8,128)(2,1)} copy(bf16[64,4096]{1,0:T(8,128)(2,1)} %get-tuple-element.8) | data formatting | bytes 1048576
  86.4 0.0 copy-done
  86.4 0.0 copy-start.2
  86.4 0.8 copy.14
  87.2 0.3 copy-done.2
  87.5 0.0 copy-start.1
  87.5 0.7 copy.15
  88.2 0.3 copy-done.1
  88.5 0.7 copy.16
Async XLA Ops:
  84.4 1.9 %copy-start = (bf16[64,4096]{1,0:T(8,128)(2,1)S(1)}, bf16[64,4096]{1,0:T(8,128)(2,1)}, u32[]{:S(2)}) copy-start(bf16[64,4096]{1,0:T(8,128)(2,1)} %get-tuple-element.9) | copy-start | bytes 1572868
  86.4 1.1 %copy-start.2 = (bf16[64,2048]{1,0:T(8,128)(2,1)S(1)}, bf16[64,2048]{1,0:T(8,128)(2,1)}, u32[]{:S(2)}) copy-start(bf16[64,2048]{1,0:T(8,128)(2,1)} %get-tuple-element.10) | copy-start | bytes 786436
  87.5 1.0 %copy-start.1 = (bf16[64,2048]{1,0:T(8,128)(2,1)S(1)}, bf16[64,2048]{1,0:T(8,128)(2,1)}, u32[]{:S(2)}) copy-start(bf16[64,2048]{1,0:T(8,128)(2,1)} %get-tuple-element.11) | copy-start | bytes 786436
